TPU v7x, 32 devices: a whole 2x2x4 slice. The times are simulated.
32 devices in a mesh: groups: 2 (over x), seq: 16 (over z, y, core).
Axes of the slice: x: 2, y: 2, z: 4, core: 2. Of those that a mesh axis runs over, the one named last changes fastest.
Arguments:
- visual: bfloat16 [32768, 1152], P(('groups', 'seq')), parts along dimension 0, may hold values from -18 to 18
- vis_proj: bfloat16 [1152, 1792], replicated, may hold values from -0.1875 to 0.1875
- kv_proj: bfloat16 [1792, 512], replicated, may hold values from -0.125 to 0.125
- out_proj: bfloat16 [1792, 1792], P(None, 'seq'), may hold values from -0.125 to 0.125
- queries: bfloat16 [256, 1792], P(('groups', 'seq')), parts along dimension 0, may hold values from -350 to 350
- frame_range: int32 [2, 2], P('groups'), parts along dimension 0, may hold values from 0 to 64, as said below
- text_lens: int32 [2], P('groups'), parts along dimension 0, may hold values from 1 to 128, as said below
Outputs:
- attended: bfloat16 [256, 1792], P(('groups', 'seq')), parts along dimension 0
There are 2 independent parts, one for each index of `groups`. A program takes and returns all parts, laid end to end along the dimension named above; an argument that names none is the same for every part. Nothing has to cross between parts.
Inputs may be any that keep to these rules, and one draw needn't show every extreme that they name: frame_range[b, 0] < frame_range[b, 1] for every block b; some block attends all 64 frames. `text_lens`: some block is full.
All inputs are finite; a program needn't handle non-finite values.
Results may differ from a plain program's by a relative error of at most 0.02.
The roundings to bfloat16 on the way count: a program that leaves them out, or rounds other values in their place, can miss the bound.
Values may be sent and summed in bfloat16 or wider, within the bound.
A program may use at most 128 MiB of HBM per device.

v0:
```python
import jax
import jax.numpy as jnp
from jax import lax
from jax.sharding import PartitionSpec as P

HEADS = 14
KV_HEADS = 2
HEAD_DIM = 128
FRAME_TOK = 256
QBLK = 128


NEG = -1e30


def fresh_state(row_count):
    return (
        jnp.zeros((row_count, HEADS * HEAD_DIM), jnp.float32),
        jnp.full((row_count, HEADS), NEG, jnp.float32),
        jnp.zeros((row_count, HEADS), jnp.float32),
    )


def absorb(running, query_rows, key_rows, value_rows, allowed):
    output_sum, maxima, totals = running
    row_count = query_rows.shape[0]
    group_size = HEADS // KV_HEADS
    query_heads = query_rows.reshape(row_count, KV_HEADS, group_size, HEAD_DIM)
    scores = jnp.einsum(
        "tkgd,rkd->tkgr", query_heads, key_rows, preferred_element_type=jnp.float32
    ) * HEAD_DIM ** (-0.5)
    masked = jnp.where(allowed, scores, NEG)
    new_maxima = jnp.maximum(maxima, jnp.max(masked, axis=-1).reshape(row_count, HEADS))
    shaped = new_maxima.reshape(row_count, KV_HEADS, group_size)
    weights = jnp.where(allowed, jnp.exp(scores - shaped[..., None]), 0.0)
    new_totals = jnp.sum(weights, axis=-1).reshape(row_count, HEADS)
    blended = jnp.einsum(
        "tkgr,rkd->tkgd",
        weights.astype(jnp.bfloat16),
        value_rows,
        preferred_element_type=jnp.float32,
    )
    new_sum = blended.reshape(row_count, HEADS, HEAD_DIM)
    return (new_sum.reshape(row_count, HEADS * HEAD_DIM), new_maxima, new_totals)


def visit_keys(running, query_rows, key_rows, value_rows, frame_range, block_id, first_row):
    local_count = key_rows.shape[0]
    bounds = lax.dynamic_index_in_dim(frame_range, block_id, 0, keepdims=False)
    frames = (first_row + jnp.arange(local_count, dtype=jnp.int32)) // FRAME_TOK
    allowed = (frames >= bounds[0]) & (frames < bounds[1])
    result = absorb(running, query_rows, key_rows, value_rows, allowed)
    return result


def body(visual, vis_proj, kv_proj, out_proj, queries, frame_range, text_lens):
    devices = lax.axis_size("seq")
    my_index = lax.axis_index("seq")
    hidden = jax.nn.gelu(
        jnp.dot(visual, vis_proj, preferred_element_type=jnp.float32), approximate=True
    ).astype(jnp.bfloat16)
    key_value = jnp.dot(hidden, kv_proj, preferred_element_type=jnp.float32).astype(jnp.bfloat16)
    kv_width = KV_HEADS * HEAD_DIM
    local_count = visual.shape[0]
    key_rows = key_value[:, :kv_width].reshape(local_count, KV_HEADS, HEAD_DIM)
    value_rows = key_value[:, kv_width:].reshape(local_count, KV_HEADS, HEAD_DIM)
    first_row = my_index * local_count
    own_count = queries.shape[0]

    def visit_local(running, query_rows, block_id):
        return visit_keys(
            running, query_rows, key_rows, value_rows, frame_range, block_id, first_row
        )

    every_query = lax.all_gather(queries, "seq", axis=0, tiled=True)
    block_count = every_query.shape[0] // QBLK
    stacked = every_query.reshape(block_count, QBLK, HEADS * HEAD_DIM)

    def one_block(packed):
        block_rows, block_id = packed
        return visit_local(fresh_state(QBLK), block_rows, block_id)

    sums_all, maxima_all, totals_all = lax.map(
        one_block, (stacked, jnp.arange(block_count, dtype=jnp.int32))
    )
    part_sums, part_maxima, part_totals = (
        lax.all_to_all(
            sums_all.reshape(1, block_count * QBLK, HEADS * HEAD_DIM),
            "seq",
            split_axis=1,
            concat_axis=0,
            tiled=True,
        ),
        lax.all_to_all(
            maxima_all.reshape(1, block_count * QBLK, HEADS),
            "seq",
            split_axis=1,
            concat_axis=0,
            tiled=True,
        ),
        lax.all_to_all(
            totals_all.reshape(1, block_count * QBLK, HEADS),
            "seq",
            split_axis=1,
            concat_axis=0,
            tiled=True,
        ),
    )
    maxima = jnp.max(part_maxima, axis=0)
    scaling = jnp.exp(part_maxima - maxima[None])
    totals = jnp.sum(scaling * part_totals, axis=0)
    weighted = part_sums.reshape(devices, own_count, HEADS, HEAD_DIM) * scaling[..., None]
    output_sum = jnp.sum(weighted, axis=0).reshape(own_count, HEADS * HEAD_DIM)
    normed = output_sum.reshape(own_count, HEADS, HEAD_DIM) / totals[..., None]
    my_block = my_index * own_count // QBLK
    length = lax.dynamic_index_in_dim(text_lens, my_block, 0, keepdims=False)
    positions = my_index * own_count % QBLK + jnp.arange(own_count, dtype=jnp.int32)
    attention = (
        jnp.where((positions < length)[:, None, None], normed, 0.0)
        .reshape(own_count, HEADS * HEAD_DIM)
        .astype(jnp.bfloat16)
    )
    return jnp.dot(
        attention,
        lax.all_gather(out_proj, "seq", axis=1, tiled=True),
        preferred_element_type=jnp.float32,
    ).astype(jnp.bfloat16)


def solution(mesh):
    placed = (
        P(("groups", "seq"), None),
        P(),
        P(),
        P(None, "seq"),
        P(("groups", "seq"), None),
        P("groups", None),
        P("groups"),
    )
    return jax.shard_map(
        body, mesh=mesh, in_specs=placed, out_specs=P(("groups", "seq"), None), check_vma=False
    )
```

profile of v0, /device:TPU:0, one launch (start us, length us, event | category | flops | bytes accessed | tf_op | source)
XLA Modules:
  0.0 116.8 jit_solution(4725177874971610116)
XLA Ops:
  6.5 0.7 all-gather.2.cloned.1.call-update
  7.3 25.8 %all_gather.6 = bf16[128,1792]{1,0:T(8,128)(2,1)S(1)} all-gather(bf16[8,1792]{1,0:T(8,128)(2,1)} %param.11), channel_id=1, replica_groups=mesh['groups'=2,'seq'=16] {'seq'}, dimensions={0}, use_global_device_ids=true | all-gather | bytes 487424 | tf_op jit(solution)/shard_map/all_gather | solution.py:75
  33.1 0.3 copy.16
  33.3 1.3 %fusion.39 = (s32[1,1]{1,0:T(1,128)}, s32[1,1]{1,0:T(1,128)}) fusion(s32[1,2]{1,0:T(1,128)} %param.12), kind=kLoop, calls=%fused_computation.51 | loop fusion | bytes 16 | tf_op jit(solution)/shard_map/while/body/eval_jaxpr/slice | solution.py:51
  34.6 1.2 %compare_and_fusion = pred[1024]{0:T(1024)(128)(4,1)S(1)} fusion(s32[]{:T(128)} %bitcast.5, s32[]{:T(128)} %bitcast.4, s32[]{:T(128)S(6)} %mul.69), kind=kLoop, calls=%fused_computation.41 | loop fusion | flops 19456 | bytes 1036 | tf_op jit(solution)/shard_map/while/body/eval_jaxpr/and | solution.py:51
  35.9 11.2 %fusion.18 = bf16[1024,512]{0,1:T(8,128)(2,1)} fusion(bf16[1792,512]{1,0:T(8,128)(2,1)} %param.9, bf16[1024,1152]{1,0:T(8,128)(2,1)S(1)} %copy-done, bf16[1152,1792]{1,0:T(8,128)(2,1)} %param.8), kind=kOutput, calls=%fused_computation.20 | convolution fusion | flops 6123945984 | bytes 9371648 | tf_op jit(solution)/shard_map/dot_general | solution.py:62
  47.1 2.1 %fusion.38 = (bf16[1024,256]{0,1:T(8,128)(2,1)S(1)}, bf16[1024,256]{0,1:T(8,128)(2,1)}) fusion(bf16[1024,512]{0,1:T(8,128)(2,1)} %fusion.18), kind=kLoop, calls=%fused_computation.50 | loop fusion | bytes 2097152 | tf_op jit(solution)/shard_map/slice | solution.py:65
  49.1 1.6 %fusion.8 = (f32[128,2,7]{0,2,1:T(8,128)S(1)}, f32[2,1024,128,7]{2,1,3,0:T(8,128)S(1)}) fusion(pred[1024]{0:T(1024)(128)(4,1)S(1)} %compare_and_fusion, bf16[1024,2,128,1]{0,2,3,1:T(8,128)(2,1)S(1)} %bitcast.58, bf16[128,2,7,128]{0,3,2,1:T(8,128)(2,1)S(1)} %bitcast.59), kind=kOutput, calls=%fused_computation.11 | convolution fusion | flops 475265280 | bytes 8331264 | tf_op jit(solution)/shard_map/while/body/eval_jaxpr/tkgd,rkd->tkgr/dot_general | solution.py:29
  50.8 2.9 %copy-done.1 = f32[2,1024,128,7]{2,1,3,0:T(8,128)} copy-done((f32[2,1024,128,7]{2,1,3,0:T(8,128)}, f32[2,1024,128,7]{2,1,3,0:T(8,128)S(1)}, u32[]{:S(2)}) %copy-start.1) | copy-done | bytes 7340056
  53.7 2.0 %fusion.11 = f32[128,2,7]{0,2,1:T(8,128)S(1)} fusion(f32[2,1024,128,7]{2,1,3,0:T(8,128)S(1)} %get-tuple-element.38, f32[128,2,7]{0,2,1:T(8,128)S(1)} %broadcast_maximum_fusion, pred[1024]{0:T(1024)(128)(4,1)S(1)} %compare_and_fusion), kind=kLoop, calls=%fused_computation.14 | loop fusion | flops 7338240 | bytes 7355392 | tf_op jit(solution)/shard_map/while/body/eval_jaxpr/reduce_sum | solution.py:36
  55.7 0.7 copy.24
  56.5 3.5 %all-to-all-start.2 = ((f32[1,128,14]{2,0,1:T(1,128)}), f32[1,128,14]{2,0,1:T(1,128)S(1)}, u32[]{:S(2)}, u32[]{:S(2)}) async-start(f32[1,128,14]{2,0,1:T(1,128)} %copy.24), calls=%async_computation.2 | async-start | bytes 131072 | tf_op jit(solution)/shard_map/all_to_all | solution.py:101
  60.0 0.7 copy.21
  60.7 6.4 %all-to-all-done.2 = f32[1,128,14]{2,0,1:T(1,128)S(1)} async-done(((f32[1,128,14]{2,0,1:T(1,128)}), f32[1,128,14]{2,0,1:T(1,128)S(1)}, u32[]{:S(2)}, u32[]{:S(2)}) %all-to-all-start.2) | async-done | bytes 7200 | tf_op jit(solution)/shard_map/all_to_all | solution.py:101
  67.1 3.7 %all-to-all-start.1 = ((f32[1,128,14]{2,0,1:T(1,128)}), f32[1,128,14]{2,0,1:T(1,128)S(1)}, u32[]{:S(2)}, u32[]{:S(2)}) async-start(f32[1,128,14]{2,0,1:T(1,128)} %copy.21), calls=%async_computation.1 | async-start | bytes 131072 | tf_op jit(solution)/shard_map/all_to_all | solution.py:94
  70.8 4.8 %fusion.13 = f32[2,128,128,7]{2,1,3,0:T(8,128)S(1)} fusion(bf16[1024,2,128,1]{0,2,3,1:T(8,128)(2,1)} %bitcast.63, f32[2,1024,128,7]{2,1,3,0:T(8,128)} %copy-done.1, f32[128,2,7]{0,2,1:T(8,128)S(1)} %broadcast_maximum_fusion, pred[1024]{0:T(1024)(128)(4,1)S(1)} %compare_and_fusion), kind=kOutput, calls=%fused_computation.16 | convolution fusion | flops 477102080 | bytes 8790016 | tf_op jit(solution)/shard_map/while/body/eval_jaxpr/tkgr,rkd->tkgd/dot_general | solution.py:37
  75.6 2.1 %copy.20 = f32[1,128,1792]{2,0,1:T(1,128)} copy(f32[1,128,1792]{1,2,0:T(8,128)S(1)} %bitcast.60) | data formatting | bytes 1835008 | tf_op jit(solution)/shard_map/while/body/jit(dynamic_update_index_in_dim)/broadcast_in_dim | solution.py:83
  77.7 5.9 %all-to-all-start = ((f32[1,128,1792]{2,0,1:T(1,128)}), f32[1,128,1792]{2,0,1:T(1,128)S(1)}, u32[]{:S(2)}, u32[]{:S(2)}) async-start(f32[1,128,1792]{2,0,1:T(1,128)} %copy.20), calls=%async_computation | async-start | bytes 1835008 | tf_op jit(solution)/shard_map/all_to_all | solution.py:87
  84.2 0.2 copy.33
  84.4 0.8 copy.32
  85.4 0.9 multiply_reduce_fusion
  86.4 18.0 %all-to-all-done = f32[1,128,1792]{2,0,1:T(1,128)S(1)} async-done(((f32[1,128,1792]{2,0,1:T(1,128)}), f32[1,128,1792]{2,0,1:T(1,128)S(1)}, u32[]{:S(2)}, u32[]{:S(2)}) %all-to-all-start) | async-done | bytes 917536 | tf_op jit(solution)/shard_map/all_to_all | solution.py:87
  104.4 0.3 fusion.21
  104.7 5.2 %convolution_convert_fusion = bf16[8,1792]{1,0:T(8,128)(2,1)} fusion(bf16[1792,1792]{0,1:T(8,128)(2,1)} %all-gather.2.cloned.1.call-done, f32[8,1792]{1,0:T(8,128)S(1)} %fusion.21, f32[8,14]{0,1:T(8,128)S(1)} %get-tuple-element.21, pred[8]{0:T(512)(128)(4,1)S(1)} %add_compare_fusion), kind=kOutput, calls=%fused_computation.19 | convolution fusion | flops 51437568 | bytes 6509000 | tf_op jit(solution)/shard_map/dot_general | solution.py:123
  (13 shorter events, 0.2 us)
Async XLA Ops:
  6.5 29.3 %copy-start = (bf16[1024,1152]{1,0:T(8,128)(2,1)S(1)}, bf16[1024,1152]{1,0:T(8,128)(2,1)}, u32[]{:S(2)}) copy-start(bf16[1024,1152]{1,0:T(8,128)(2,1)} %param.7) | copy-start | bytes 7077892
  6.5 98.2 %all-gather.2.cloned.1.call-start = ((), (), s32[]{:S(2)}) async-start(), calls=%async_computation.3 | async-start | bytes 6823936 | tf_op jit(solution)/shard_map/all_gather | solution.py:125
  50.8 3.0 %copy-start.1 = (f32[2,1024,128,7]{2,1,3,0:T(8,128)}, f32[2,1024,128,7]{2,1,3,0:T(8,128)S(1)}, u32[]{:S(2)}) copy-start(f32[2,1024,128,7]{2,1,3,0:T(8,128)S(1)} %get-tuple-element.38) | copy-start | bytes 22020100
  56.5 10.7 %all-to-all-start.2 = ((f32[1,128,14]{2,0,1:T(1,128)}), f32[1,128,14]{2,0,1:T(1,128)S(1)}, u32[]{:S(2)}, u32[]{:S(2)}) async-start(f32[1,128,14]{2,0,1:T(1,128)} %copy.24), calls=%async_computation.2 | async-start | bytes 131072 | tf_op jit(solution)/shard_map/all_to_all | solution.py:101
  67.1 10.6 %all-to-all-start.1 = ((f32[1,128,14]{2,0,1:T(1,128)}), f32[1,128,14]{2,0,1:T(1,128)S(1)}, u32[]{:S(2)}, u32[]{:S(2)}) async-start(f32[1,128,14]{2,0,1:T(1,128)} %copy.21), calls=%async_computation.1 | async-start | bytes 131072 | tf_op jit(solution)/shard_map/all_to_all | solution.py:94
  77.7 26.7 %all-to-all-start = ((f32[1,128,1792]{2,0,1:T(1,128)}), f32[1,128,1792]{2,0,1:T(1,128)S(1)}, u32[]{:S(2)}, u32[]{:S(2)}) async-start(f32[1,128,1792]{2,0,1:T(1,128)} %copy.20), calls=%async_computation | async-start | bytes 1835008 | tf_op jit(solution)/shard_map/all_to_all | solution.py:87
Sparse Core Ops, SparseCore 0:
  9.6 66.3 all-gather.1
where the time goes:
time: 118 us; the launch traced here: 117 us
  blocking collectives  25.8 us (22%)
  waiting for transfers between devices  25.2 us (21%)
  matrix products  22.8 us (19%)
  between operations  14.2 us (12%)
  starting transfers between devices  13 us (11%)
  local copies, waits for them, and re-layouts  11.3 us (10%)
  other arithmetic  4.46 us (4%)
    all_gather x1, blocking collectives, body(): every_query = lax.all_gather(queries, 'seq', axis=0, tiled=True)  25.8 us
    all_to_all x1, waiting for transfers between devices, body(): lax.all_to_all(sums_all.reshape(1, block_count * QBLK, HEADS * HEAD_DIM),...  18 us
    dot_general x1, matrix products, body(): jnp.dot(hidden, kv_proj, preferred_element_type=jnp.float32)  11.2 us
    all_to_all x1, waiting for transfers between devices, body(): lax.all_to_all(totals_all.reshape(1, block_count * QBLK, HEADS), 'seq', s...  6.42 us
    all_to_all x1, starting transfers between devices, body(): lax.all_to_all(sums_all.reshape(1, block_count * QBLK, HEADS * HEAD_DIM),...  5.87 us
    dot_general x1, matrix products, body(): jnp.dot(attention, lax.all_gather(out_proj, 'seq', axis=1, tiled=True), p...  5.24 us
    dot_general x1, matrix products, absorb(): jnp.einsum('tkgr,rkd->tkgd', weights.astype(jnp.bfloat16), value_rows, pr...  4.78 us
    all_to_all x1, starting transfers between devices, body(): lax.all_to_all(maxima_all.reshape(1, block_count * QBLK, HEADS), 'seq', s...  3.67 us
  transfers between devices with their start and end apart: 4, of which 2 were waited for; matrix products, arithmetic and copies ran while one was open for 26% of the time, Pallas kernels for 0%

commit v1 on v0

v1 whole, which is shorter than its diff:
```python
import functools
import math

import jax
import jax.numpy as jnp
from jax import lax
from jax.experimental import pallas as pl
from jax.experimental.pallas import tpu as pltpu
from jax.sharding import PartitionSpec as P

HEADS = 14
KV_HEADS = 2
GROUP = HEADS // KV_HEADS
HEAD_DIM = 128
FRAME_TOK = 256
QBLK = 128
HALF = GROUP * HEAD_DIM
INNER = 4
COLS = 256
ROWS = 256
NEG = -1e30
FLOOR = -1e29
EXP_SCALE = HEAD_DIM ** (-0.5) * math.log2(math.e)
GELU_SCALE = math.sqrt(2.0 / math.pi)
MESH = pl.DeviceIdType.MESH


def gelu(v):
    return 0.5 * v * (1.0 + jnp.tanh(GELU_SCALE * (v + 0.044715 * (v * v * v))))


def kernel(
    n,
    vis_hbm,
    vp_hbm,
    kvp_hbm,
    wo_hbm,
    q_ref,
    range_ref,
    lens_ref,
    out_ref,
    vis,
    vp,
    kvp,
    wbuf,
    hidden,
    kvbuf,
    kvsend,
    qbuf,
    nums,
    numrecv,
    stats,
    statrecv,
    attn,
    yb,
    yrecv,
    load_sem,
    vp_sem,
    w_send,
    w_recv,
    kv_send,
    kv_recv,
    q_send,
    q_recv,
    n_send,
    n_recv,
    s_send,
    s_recv,
    a_send,
    a_recv,
    y_send,
    y_recv,
):
    me = lax.axis_index("seq")
    core = lax.rem(me, 2)
    other = 1 - core
    sibling = me + 1 - 2 * core
    inner = lax.rem(me, INNER)
    outer = lax.div(me, INNER)
    base = me - inner
    across_slot = lax.rem(inner + 2, INNER)
    across = base + across_slot
    sibling_slot = sibling - base
    last_slot = lax.rem(sibling_slot + 2, INNER)
    outers = n // INNER
    own = q_ref.shape[0]
    local = vis.shape[0]
    width = vp.shape[1]
    chunks = width // COLS
    blocks = n * own // QBLK
    per_block = QBLK // own

    vis_copy = pltpu.make_async_copy(vis_hbm, vis, load_sem.at[0])
    vis_copy.start()

    def vp_copy(j):
        cols = pl.ds(pl.multiple_of(j * COLS, COLS), COLS)
        return pltpu.make_async_copy(vp_hbm.at[:, cols], vp.at[:, cols], vp_sem.at[j])

    vp_copy(0).start()
    w_copy = pltpu.make_async_copy(wo_hbm, wbuf.at[inner], load_sem.at[1])
    w_copy.start()
    for j in range(1, chunks):
        vp_copy(j).start()
    kvp_copy = pltpu.make_async_copy(kvp_hbm, kvp, load_sem.at[2])
    kvp_copy.start()

    barrier = pltpu.get_barrier_semaphore()

    @pl.loop(1, n)
    def _(i):
        pl.semaphore_signal(
            barrier, inc=1, device_id={"seq": lax.rem(me + i, n)}, device_id_type=MESH
        )

    def remote(src, dst, send, recv, peer):
        return pltpu.make_async_remote_copy(
            src_ref=src,
            dst_ref=dst,
            send_sem=send,
            recv_sem=recv,
            device_id={"seq": peer},
            device_id_type=MESH,
        )

    def hidden_chunk(j):
        vp_copy(j).wait()
        cols = pl.ds(pl.multiple_of(j * COLS, COLS), COLS)
        for r in range(local // ROWS):
            rows = pl.ds(r * ROWS, ROWS)
            value = jnp.dot(vis[rows, :], vp[:, cols], preferred_element_type=jnp.float32)
            hidden[rows, cols] = gelu(value).astype(jnp.bfloat16)

    vis_copy.wait()
    hidden_chunk(0)

    pl.semaphore_wait(barrier, n - 1)

    def q_copy(peer, slot, index):
        head = pl.ds(pl.multiple_of(lax.rem(peer, 2) * HALF, HEAD_DIM), HALF)
        return remote(q_ref.at[:, head], qbuf.at[slot], q_send.at[index], q_recv.at[slot], peer)

    @pl.loop(1, n)
    def _(i):
        q_copy(lax.rem(me + i, n), me, i).start()

    w_copy.wait()
    w_across = remote(
        wbuf.at[inner], wbuf.at[inner], w_send.at[0], w_recv.at[inner], across
    )
    w_sibling = remote(
        wbuf.at[inner], wbuf.at[inner], w_send.at[1], w_recv.at[inner], sibling
    )
    w_across.start()
    w_sibling.start()
    qbuf[me] = q_ref[:, pl.ds(pl.multiple_of(core * HALF, HEAD_DIM), HALF)]

    @pl.loop(1, chunks)
    def _(j):
        hidden_chunk(j)

    kvp_copy.wait()

    def project(head, store):
        keys = pl.ds(pl.multiple_of(head * HEAD_DIM, HEAD_DIM), HEAD_DIM)
        values = pl.ds(
            pl.multiple_of((KV_HEADS + head) * HEAD_DIM, HEAD_DIM), HEAD_DIM
        )
        weights = jnp.concatenate([kvp[:, keys], kvp[:, values]], axis=1)
        for r in range(local // ROWS):
            rows = pl.ds(r * ROWS, ROWS)
            both = jnp.dot(
                hidden[rows, :], weights, preferred_element_type=jnp.float32
            ).astype(jnp.bfloat16)
            store(rows, both[:, :HEAD_DIM], both[:, HEAD_DIM:])

    def store_send(rows, keys, values):
        kvsend[0, rows, :] = keys
        kvsend[1, rows, :] = values

    def store_own(rows, keys, values):
        kvbuf[0, 0, rows, :] = keys
        kvbuf[0, 1, rows, :] = values

    project(other, store_send)
    kv_copy = remote(kvsend, kvbuf.at[1], kv_send, kv_recv, sibling)
    kv_copy.start()
    project(core, store_own)

    def w_arrival(slot):
        return remote(wbuf.at[slot], wbuf.at[slot], w_send.at[2], w_recv.at[slot], sibling)

    w_arrival(across_slot).wait_recv()
    w_forward = w_arrival(across_slot)
    w_forward.start()

    @pl.loop(1, n)
    def _(i):
        peer = lax.rem(me + i, n)
        q_copy(peer, peer, i).wait_recv()

    kv_copy.wait_recv()

    lane = lax.broadcasted_iota(jnp.int32, (QBLK, HEAD_DIM), 1)
    token = lax.broadcasted_iota(jnp.int32, (1, local), 1)
    for b in range(blocks):
        owners = pl.ds(b * per_block, per_block)
        low = range_ref[b, 0] * FRAME_TOK
        high = range_ref[b, 1] * FRAME_TOK
        allowed = []
        for device in (me, sibling):
            row = token + device * local
            allowed.append((row >= low) & (row < high))
        stat = jnp.zeros((QBLK, HEAD_DIM), jnp.float32)
        for h in range(GROUP):
            cols = pl.ds(h * HEAD_DIM, HEAD_DIM)
            query = (
                qbuf[owners, :, cols]
                .astype(jnp.float32)
                .reshape(QBLK, HEAD_DIM)
                .astype(jnp.bfloat16)
            )
            scores = []
            for slot in range(2):
                raw = lax.dot_general(
                    query,
                    kvbuf[slot, 0],
                    (((1,), (1,)), ((), ())),
                    preferred_element_type=jnp.float32,
                )
                scores.append(jnp.where(allowed[slot], raw, NEG))
            top = jnp.maximum(
                jnp.max(jnp.maximum(scores[0], scores[1]), axis=1, keepdims=True), FLOOR
            )
            weights = [jnp.exp2((s - top) * EXP_SCALE) for s in scores]
            total = jnp.sum(weights[0] + weights[1], axis=1, keepdims=True)
            numer = jnp.dot(
                weights[0].astype(jnp.bfloat16),
                kvbuf[0, 1],
                preferred_element_type=jnp.float32,
            ) + jnp.dot(
                weights[1].astype(jnp.bfloat16),
                kvbuf[1, 1],
                preferred_element_type=jnp.float32,
            )
            nums[owners, :, cols] = numer.reshape(per_block, own, HEAD_DIM).astype(
                jnp.bfloat16
            )
            stat = jnp.where(lane == h, top, stat)
            stat = jnp.where(lane == h + HEAD_DIM // 2, total, stat)
        stats[owners] = stat.reshape(per_block, own, HEAD_DIM)

    def n_copy(row_owner, slot, peer, index):
        return remote(
            nums.at[row_owner], numrecv.at[slot], n_send.at[index], n_recv.at[slot], peer
        )

    def s_copy(row_owner, slot, peer, index):
        return remote(
            stats.at[row_owner], statrecv.at[slot], s_send.at[index], s_recv.at[slot], peer
        )

    @pl.loop(1, n)
    def _(i):
        peer = lax.rem(me + i, n)
        s_copy(peer, me, peer, i).start()
        n_copy(peer, me, peer, i).start()

    numrecv[me] = nums[me]
    statrecv[me] = stats[me]

    @pl.loop(1, n)
    def _(i):
        peer = lax.rem(me + i, n)
        s_copy(peer, peer, peer, i).wait_recv()
        n_copy(peer, peer, peer, i).wait_recv()

    length = lens_ref[lax.div(me * own, QBLK)]
    position = lax.rem(me * own, QBLK) + lax.broadcasted_iota(jnp.int32, (own, HEAD_DIM), 0)
    valid = position < length
    for k in range(KV_HEADS):
        sources = range(k, n, KV_HEADS)
        top = functools.reduce(jnp.maximum, [statrecv[s] for s in sources])
        factors = [jnp.exp2((statrecv[s] - top) * EXP_SCALE) for s in sources]
        totals = functools.reduce(
            jnp.add,
            [
                f * pltpu.roll(statrecv[s], HEAD_DIM // 2, 1)
                for f, s in zip(factors, sources)
            ],
        )
        for h in range(GROUP):
            cols = pl.ds(h * HEAD_DIM, HEAD_DIM)
            sums = functools.reduce(
                jnp.add,
                [
                    numrecv[s, :, cols].astype(jnp.float32) * f[:, h : h + 1]
                    for f, s in zip(factors, sources)
                ],
            )
            normed = jnp.where(valid, sums / totals[:, h : h + 1], 0.0)
            attn[outer, :, pl.ds(k * HALF + h * HEAD_DIM, HEAD_DIM)] = normed.astype(
                jnp.bfloat16
            )

    def a_copy(slot, peer_outer, index):
        return remote(
            attn.at[slot],
            attn.at[slot],
            a_send.at[index],
            a_recv.at[slot],
            peer_outer * INNER + inner,
        )

    for i in range(1, outers):
        a_copy(outer, lax.rem(outer + i, outers), i).start()
    w_arrival(sibling_slot).wait_recv()
    w_arrival(last_slot).wait_recv()
    for i in range(1, outers):
        peer_outer = lax.rem(outer + i, outers)
        a_copy(peer_outer, peer_outer, i).wait_recv()

    rows = (
        attn[...]
        .astype(jnp.float32)
        .reshape(outers * own, HEADS * HEAD_DIM)
        .astype(jnp.bfloat16)
    )
    for j in range(INNER):
        product = jnp.dot(rows, wbuf[j], preferred_element_type=jnp.float32)
        yb[:, j] = product.reshape(outers, own, product.shape[1]).astype(jnp.bfloat16)

    def y_copy(row_outer, slot, peer_outer, index):
        return remote(
            yb.at[row_outer],
            yrecv.at[slot],
            y_send.at[index],
            y_recv.at[slot],
            peer_outer * INNER + inner,
        )

    for i in range(1, outers):
        peer_outer = lax.rem(outer + i, outers)
        y_copy(peer_outer, outer, peer_outer, i).start()
    yrecv[outer] = yb[outer]

    w_across.wait_send()
    w_sibling.wait_send()
    w_forward.wait_send()
    kv_copy.wait_send()

    @pl.loop(1, n)
    def _(i):
        peer = lax.rem(me + i, n)
        q_copy(peer, me, i).wait_send()
        s_copy(peer, me, peer, i).wait_send()
        n_copy(peer, me, peer, i).wait_send()

    for i in range(1, outers):
        peer_outer = lax.rem(outer + i, outers)
        a_copy(outer, peer_outer, i).wait_send()
        y_copy(peer_outer, peer_outer, peer_outer, i).wait_recv()
    for i in range(1, outers):
        peer_outer = lax.rem(outer + i, outers)
        y_copy(peer_outer, outer, peer_outer, i).wait_send()
    out_ref[...] = yrecv[...]


def body(visual, vis_proj, kv_proj, out_proj, queries, frame_range, text_lens):
    n = lax.axis_size("seq")
    own = queries.shape[0]
    local = visual.shape[0]
    outers = n // INNER
    cols = out_proj.shape[1]
    low = jnp.bfloat16
    dma = pltpu.SemaphoreType.DMA
    hbm = pl.BlockSpec(memory_space=pl.ANY)
    smem = pl.BlockSpec(memory_space=pltpu.SMEM)
    vmem = pl.BlockSpec(memory_space=pltpu.VMEM)
    result = pl.pallas_call(
        functools.partial(kernel, n),
        out_shape=jax.ShapeDtypeStruct((outers, INNER, own, cols), low),
        in_specs=[hbm, hbm, hbm, hbm, vmem, smem, smem],
        out_specs=vmem,
        scratch_shapes=[
            pltpu.VMEM(visual.shape, low),
            pltpu.VMEM(vis_proj.shape, low),
            pltpu.VMEM(kv_proj.shape, low),
            pltpu.VMEM((INNER,) + out_proj.shape, low),
            pltpu.VMEM((local, vis_proj.shape[1]), low),
            pltpu.VMEM((2, 2, local, HEAD_DIM), low),
            pltpu.VMEM((2, local, HEAD_DIM), low),
            pltpu.VMEM((n, own, HALF), low),
            pltpu.VMEM((n, own, HALF), low),
            pltpu.VMEM((n, own, HALF), low),
            pltpu.VMEM((n, own, HEAD_DIM), jnp.float32),
            pltpu.VMEM((n, own, HEAD_DIM), jnp.float32),
            pltpu.VMEM((outers, own, HEADS * HEAD_DIM), low),
            pltpu.VMEM((outers, INNER, own, cols), low),
            pltpu.VMEM((outers, INNER, own, cols), low),
            dma((3,)),
            dma((vis_proj.shape[1] // COLS,)),
            dma((3,)),
            dma((INNER,)),
            dma,
            dma,
            dma((n,)),
            dma((n,)),
            dma((n,)),
            dma((n,)),
            dma((n,)),
            dma((n,)),
            dma((outers,)),
            dma((outers,)),
            dma((outers,)),
            dma((outers,)),
        ],
        compiler_params=pltpu.CompilerParams(
            collective_id=0, has_side_effects=True, vmem_limit_bytes=56 * 1024 * 1024
        ),
        name="layer",
    )(visual, vis_proj, kv_proj, out_proj, queries, frame_range, text_lens)
    return jnp.transpose(result.reshape(n, own, cols), (1, 0, 2)).reshape(own, n * cols)


def solution(mesh):
    placed = (
        P(("groups", "seq"), None),
        P(),
        P(),
        P(None, "seq"),
        P(("groups", "seq"), None),
        P("groups", None),
        P("groups"),
    )
    return jax.shard_map(
        body, mesh=mesh, in_specs=placed, out_specs=P(("groups", "seq"), None), check_vma=False
    )
```

time: 118 us -> 47.5 us (0.40)
  Pallas kernels: 0 us -> 43.1 us
  blocking collectives: 25.8 us -> 0 us
  waiting for transfers between devices: 25.2 us -> 0 us
  matrix products: 22.8 us -> 0 us
  between operations: 14.2 us -> 0.66 us
  starting transfers between devices: 13 us -> 0 us
  local copies, waits for them, and re-layouts: 11.3 us -> 3.46 us
  other arithmetic: 4.46 us -> 0 us
    pallas_call x0 -> x1, Pallas kernels: none -> 43.1 us  [body(): pl.pallas_call(functools.partial(kernel, n), out_shape=jax.ShapeDtypeStru...]
    all_gather x1 -> x0, blocking collectives: 25.8 us -> none  [body(): every_query = lax.all_gather(queries, 'seq', axis=0, tiled=True)]
    all_to_all x3 -> x0, waiting for transfers between devices: 24.4 us -> none  [the longest x1 18 us: body(): lax.all_to_all(sums_all.reshape(1, block_count * QBLK, HEADS * HEAD_DIM),...]
    dot_general x4 -> x0, matrix products: 22.8 us -> none  [the longest x1 11.2 us: body(): jnp.dot(hidden, kv_proj, preferred_element_type=jnp.float32)]
    all_to_all x3 -> x0, starting transfers between devices: 13 us -> none  [the longest x1 5.87 us: body(): lax.all_to_all(sums_all.reshape(1, block_count * QBLK, HEADS * HEAD_DIM),...]
    broadcast_in_dim x5 -> x0, local copies, waits for them, and re-layouts: 3.57 us -> none  [the longest x3 2.83 us: body(): lax.map(one_block, (stacked, jnp.arange(block_count, dtype=jnp.int32)))]
    slice x2 -> x0, local copies, waits for them, and re-layouts: 3.38 us -> none  [the longest x1 2.07 us: body(): key_rows = key_value[:, :kv_width].reshape(local_count, KV_HEADS, HEAD_DIM)]
    reduce_sum x3 -> x0, other arithmetic: 3.21 us -> none  [the longest x1 1.97 us: absorb(): new_totals = jnp.sum(weights, axis=-1).reshape(row_count, HEADS)]
  transfers between devices with their start and end apart: 4 -> 0, of which waited for: 2 -> 0; matrix products, arithmetic and copies ran while one was open for 26% -> 0% of each run, Pallas kernels for 0% -> 0%
where the time goes in v1:
time: 47.5 us; the launch traced here: 47.2 us
  Pallas kernels  43.1 us (91%)
  local copies, waits for them, and re-layouts  3.46 us (7%)
  between operations  0.66 us (1%)
    pallas_call x1, Pallas kernels, body(): pl.pallas_call(functools.partial(kernel, n), out_shape=jax.ShapeDtypeStru...  43.1 us
    unnamed x1, local copies, waits for them, and re-layouts  1.98 us

profile of v1, /device:TPU:0, one launch (start us, length us, event | category | flops | bytes accessed | tf_op | source)
XLA Modules:
  0.0 47.2 jit_solution(8251020282978933094)
XLA Ops:
  0.7 2.0 %copy.8.wo_hbm = bf16[1792,112]{1,0:T(8,128)(2,1)} copy(bf16[1792,112]{0,1:T(8,128)(2,1)} %param.10) | data formatting | bytes 802816 | tf_op args[3]
  2.6 43.1 %layer.1 = bf16[4,4,8,112]{3,2,1,0:T(8,128)(2,1)} custom-call(bf16[1024,1152]{1,0:T(8,128)(2,1)} %vis_hbm.1, bf16[1152,1792]{1,0:T(8,128)(2,1)} %vp_hbm.1, bf16[1792,512]{1,0:T(8,128)(2,1)} %kvp_hbm.1, bf16[1792,112]{1,0:T(8,128)(2,1)} %copy.8.wo_hbm, bf16[8,1792]{1,0:T(8,128)(2,1)} %q_ref.1, s32[1,2]{1,0:T(1,128)} %range_ref.1, s32[1]{0:T(128)S(6)} %copy.10.lens_ref), custom_call_target="tpu_custom_call" | custom-call | tf_op jit(solution)/shard_map/layer/pallas_call | solution.py:380
  45.7 0.8 %copy.9 = bf16[8,16,112]{2,1,0:T(8,128)(2,1)S(1)} copy(bf16[8,16,112]{2,0,1:T(8,128)(2,1)} %bitcast.3) | data formatting | bytes 57344 | tf_op jit(solution)/shard_map/transpose | solution.py:423
  46.5 0.7 %reshape.7 = bf16[8,1792]{1,0:T(8,128)(2,1)} reshape(bf16[8,16,112]{2,1,0:T(8,128)(2,1)S(1)} %copy.9) | data formatting | bytes 57344 | tf_op jit(solution)/shard_map/reshape | solution.py:423

commit v2 on v1

--- a/solution.py
+++ b/solution.py
@@ -22,11 +22,14 @@
 FLOOR = -1e29
 EXP_SCALE = HEAD_DIM ** (-0.5) * math.log2(math.e)
 GELU_SCALE = math.sqrt(2.0 / math.pi)
+GELU_CUBE = 0.044715 * GELU_SCALE
+SPLIT = 4
 MESH = pl.DeviceIdType.MESH
 
 
 def gelu(v):
-    return 0.5 * v * (1.0 + jnp.tanh(GELU_SCALE * (v + 0.044715 * (v * v * v))))
+    half = 0.5 * v
+    return half + half * jnp.tanh(v * (GELU_SCALE + GELU_CUBE * (v * v)))
 
 
 def kernel(
@@ -190,10 +193,6 @@
     def w_arrival(slot):
         return remote(wbuf.at[slot], wbuf.at[slot], w_send.at[2], w_recv.at[slot], sibling)
 
-    w_arrival(across_slot).wait_recv()
-    w_forward = w_arrival(across_slot)
-    w_forward.start()
-
     @pl.loop(1, n)
     def _(i):
         peer = lax.rem(me + i, n)
@@ -203,17 +202,33 @@
 
     lane = lax.broadcasted_iota(jnp.int32, (QBLK, HEAD_DIM), 1)
     token = lax.broadcasted_iota(jnp.int32, (1, local), 1)
+    def n_copy(row_owner, slot, peer, index, part):
+        cols = pl.ds(0, SPLIT * HEAD_DIM) if part == 0 else pl.ds(SPLIT * HEAD_DIM, HALF - SPLIT * HEAD_DIM)
+        return remote(
+            nums.at[row_owner, :, cols],
+            numrecv.at[slot, :, cols],
+            n_send.at[part, index],
+            n_recv.at[part, slot],
+            peer,
+        )
+
+    def s_copy(row_owner, slot, peer, index):
+        return remote(
+            stats.at[row_owner], statrecv.at[slot], s_send.at[index], s_recv.at[slot], peer
+        )
+
+    allowed = []
     for b in range(blocks):
-        owners = pl.ds(b * per_block, per_block)
         low = range_ref[b, 0] * FRAME_TOK
         high = range_ref[b, 1] * FRAME_TOK
-        allowed = []
         for device in (me, sibling):
             row = token + device * local
             allowed.append((row >= low) & (row < high))
-        stat = jnp.zeros((QBLK, HEAD_DIM), jnp.float32)
-        for h in range(GROUP):
-            cols = pl.ds(h * HEAD_DIM, HEAD_DIM)
+    stat = [jnp.zeros((QBLK, HEAD_DIM), jnp.float32)] * blocks
+    for h in range(GROUP):
+        cols = pl.ds(h * HEAD_DIM, HEAD_DIM)
+        for b in range(blocks):
+            owners = pl.ds(b * per_block, per_block)
             query = (
                 qbuf[owners, :, cols]
                 .astype(jnp.float32)
@@ -228,7 +243,7 @@
                     (((1,), (1,)), ((), ())),
                     preferred_element_type=jnp.float32,
                 )
-                scores.append(jnp.where(allowed[slot], raw, NEG))
+                scores.append(jnp.where(allowed[2 * b + slot], raw, NEG))
             top = jnp.maximum(
                 jnp.max(jnp.maximum(scores[0], scores[1]), axis=1, keepdims=True), FLOOR
             )
@@ -246,25 +261,27 @@
             nums[owners, :, cols] = numer.reshape(per_block, own, HEAD_DIM).astype(
                 jnp.bfloat16
             )
-            stat = jnp.where(lane == h, top, stat)
-            stat = jnp.where(lane == h + HEAD_DIM // 2, total, stat)
-        stats[owners] = stat.reshape(per_block, own, HEAD_DIM)
-
-    def n_copy(row_owner, slot, peer, index):
-        return remote(
-            nums.at[row_owner], numrecv.at[slot], n_send.at[index], n_recv.at[slot], peer
-        )
-
-    def s_copy(row_owner, slot, peer, index):
-        return remote(
-            stats.at[row_owner], statrecv.at[slot], s_send.at[index], s_recv.at[slot], peer
-        )
+            stat[b] = jnp.where(lane == h, top, stat[b])
+            stat[b] = jnp.where(lane == h + HEAD_DIM // 2, total, stat[b])
+        if h == SPLIT - 1:
+
+            @pl.loop(1, n)
+            def _(i):
+                peer = lax.rem(me + i, n)
+                n_copy(peer, me, peer, i, 0).start()
+
+    for b in range(blocks):
+        stats[pl.ds(b * per_block, per_block)] = stat[b].reshape(per_block, own, HEAD_DIM)
 
     @pl.loop(1, n)
     def _(i):
         peer = lax.rem(me + i, n)
         s_copy(peer, me, peer, i).start()
-        n_copy(peer, me, peer, i).start()
+        n_copy(peer, me, peer, i, 1).start()
+
+    w_arrival(across_slot).wait_recv()
+    w_forward = w_arrival(across_slot)
+    w_forward.start()
 
     numrecv[me] = nums[me]
     statrecv[me] = stats[me]
@@ -273,11 +290,22 @@
     def _(i):
         peer = lax.rem(me + i, n)
         s_copy(peer, peer, peer, i).wait_recv()
-        n_copy(peer, peer, peer, i).wait_recv()
+        n_copy(peer, peer, peer, i, 0).wait_recv()
+        n_copy(peer, peer, peer, i, 1).wait_recv()
 
     length = lens_ref[lax.div(me * own, QBLK)]
     position = lax.rem(me * own, QBLK) + lax.broadcasted_iota(jnp.int32, (own, HEAD_DIM), 0)
     valid = position < length
+    def a_copy(slot, peer_outer, index, part):
+        cols = pl.ds(part * HALF, HALF)
+        return remote(
+            attn.at[slot, :, cols],
+            attn.at[slot, :, cols],
+            a_send.at[part, index],
+            a_recv.at[part, slot],
+            peer_outer * INNER + inner,
+        )
+
     for k in range(KV_HEADS):
         sources = range(k, n, KV_HEADS)
         top = functools.reduce(jnp.maximum, [statrecv[s] for s in sources])
@@ -302,33 +330,35 @@
             attn[outer, :, pl.ds(k * HALF + h * HEAD_DIM, HEAD_DIM)] = normed.astype(
                 jnp.bfloat16
             )
-
-    def a_copy(slot, peer_outer, index):
-        return remote(
-            attn.at[slot],
-            attn.at[slot],
-            a_send.at[index],
-            a_recv.at[slot],
-            peer_outer * INNER + inner,
-        )
-
-    for i in range(1, outers):
-        a_copy(outer, lax.rem(outer + i, outers), i).start()
+        for i in range(1, outers):
+            a_copy(outer, lax.rem(outer + i, outers), i, k).start()
+
     w_arrival(sibling_slot).wait_recv()
     w_arrival(last_slot).wait_recv()
-    for i in range(1, outers):
-        peer_outer = lax.rem(outer + i, outers)
-        a_copy(peer_outer, peer_outer, i).wait_recv()
-
-    rows = (
-        attn[...]
-        .astype(jnp.float32)
-        .reshape(outers * own, HEADS * HEAD_DIM)
-        .astype(jnp.bfloat16)
-    )
+    product = None
+    for k in range(KV_HEADS):
+        for i in range(1, outers):
+            peer_outer = lax.rem(outer + i, outers)
+            a_copy(peer_outer, peer_outer, i, k).wait_recv()
+        cols = pl.ds(k * HALF, HALF)
+        rows = (
+            attn[:, :, cols]
+            .astype(jnp.float32)
+            .reshape(outers * own, HALF)
+            .astype(jnp.bfloat16)
+        )
+        terms = [
+            lax.dot_general(
+                rows,
+                wbuf[j, :, cols],
+                (((1,), (1,)), ((), ())),
+                preferred_element_type=jnp.float32,
+            )
+            for j in range(INNER)
+        ]
+        product = terms if k == 0 else [a + b for a, b in zip(product, terms)]
     for j in range(INNER):
-        product = jnp.dot(rows, wbuf[j], preferred_element_type=jnp.float32)
-        yb[:, j] = product.reshape(outers, own, product.shape[1]).astype(jnp.bfloat16)
+        yb[:, j] = product[j].reshape(outers, own, product[j].shape[1]).astype(jnp.bfloat16)
 
     def y_copy(row_outer, slot, peer_outer, index):
         return remote(
@@ -354,16 +384,21 @@
         peer = lax.rem(me + i, n)
         q_copy(peer, me, i).wait_send()
         s_copy(peer, me, peer, i).wait_send()
-        n_copy(peer, me, peer, i).wait_send()
+        n_copy(peer, me, peer, i, 0).wait_send()
+        n_copy(peer, me, peer, i, 1).wait_send()
 
     for i in range(1, outers):
         peer_outer = lax.rem(outer + i, outers)
-        a_copy(outer, peer_outer, i).wait_send()
+        a_copy(outer, peer_outer, i, 0).wait_send()
+        a_copy(outer, peer_outer, i, 1).wait_send()
         y_copy(peer_outer, peer_outer, peer_outer, i).wait_recv()
     for i in range(1, outers):
         peer_outer = lax.rem(outer + i, outers)
         y_copy(peer_outer, outer, peer_outer, i).wait_send()
-    out_ref[...] = yrecv[...]
+    pieces = [
+        yrecv[o, j].astype(jnp.float32) for o in range(outers) for j in range(INNER)
+    ]
+    out_ref[...] = jnp.concatenate(pieces, axis=1).astype(jnp.bfloat16)
 
 
 def body(visual, vis_proj, kv_proj, out_proj, queries, frame_range, text_lens):
@@ -379,14 +414,14 @@
     vmem = pl.BlockSpec(memory_space=pltpu.VMEM)
     result = pl.pallas_call(
         functools.partial(kernel, n),
-        out_shape=jax.ShapeDtypeStruct((outers, INNER, own, cols), low),
+        out_shape=jax.ShapeDtypeStruct((own, n * cols), low),
         in_specs=[hbm, hbm, hbm, hbm, vmem, smem, smem],
         out_specs=vmem,
         scratch_shapes=[
             pltpu.VMEM(visual.shape, low),
             pltpu.VMEM(vis_proj.shape, low),
             pltpu.VMEM(kv_proj.shape, low),
-            pltpu.VMEM((INNER,) + out_proj.shape, low),
+            pltpu.VMEM((INNER, cols, out_proj.shape[0]), low),
             pltpu.VMEM((local, vis_proj.shape[1]), low),
             pltpu.VMEM((2, 2, local, HEAD_DIM), low),
             pltpu.VMEM((2, local, HEAD_DIM), low),
@@ -406,12 +441,12 @@
             dma,
             dma((n,)),
             dma((n,)),
+            dma((2, n)),
+            dma((2, n)),
             dma((n,)),
             dma((n,)),
-            dma((n,)),
-            dma((n,)),
-            dma((outers,)),
-            dma((outers,)),
+            dma((2, outers)),
+            dma((2, outers)),
             dma((outers,)),
             dma((outers,)),
         ],
@@ -419,8 +454,8 @@
             collective_id=0, has_side_effects=True, vmem_limit_bytes=56 * 1024 * 1024
         ),
         name="layer",
-    )(visual, vis_proj, kv_proj, out_proj, queries, frame_range, text_lens)
-    return jnp.transpose(result.reshape(n, own, cols), (1, 0, 2)).reshape(own, n * cols)
+    )(visual, vis_proj, kv_proj, out_proj.T, queries, frame_range, text_lens)
+    return result
 
 
 def solution(mesh):

time: 47.5 us -> 40 us (0.84)
  Pallas kernels: 43.1 us -> 37.7 us
  local copies, waits for them, and re-layouts: 3.46 us -> 1.36 us
    pallas_call x1, Pallas kernels: 43.1 us -> 37.7 us  [body(): pl.pallas_call(functools.partial(kernel, n), out_shape=jax.ShapeDtypeStru...]
    transpose x1 -> x0, local copies, waits for them, and re-layouts: 0.77 us -> none  [body(): jnp.transpose(result.reshape(n, own, cols), (1, 0, 2))]
    reshape x1 -> x0, local copies, waits for them, and re-layouts: 0.72 us -> none  [body(): jnp.transpose(result.reshape(n, own, cols), (1, 0, 2))]
    unnamed x1, local copies, waits for them, and re-layouts: 1.98 us -> 1.36 us
where the time goes in v2:
time: 40 us; the launch traced here: 39.7 us
  Pallas kernels  37.7 us (94%)
  local copies, waits for them, and re-layouts  1.36 us (3%)
  between operations  0.66 us (2%)
    pallas_call x1, Pallas kernels, body(): pl.pallas_call(functools.partial(kernel, n), out_shape=jax.ShapeDtypeStru...  37.7 us
    unnamed x1, local copies, waits for them, and re-layouts  1.36 us

profile of v2, /device:TPU:0, one launch (start us, length us, event | category | flops | bytes accessed | tf_op | source)
XLA Modules:
  0.0 39.7 jit_solution(14581495167630566874)
XLA Ops:
  0.7 37.7 %layer.1 = bf16[8,1792]{1,0:T(8,128)(2,1)} custom-call(bf16[1024,1152]{1,0:T(8,128)(2,1)} %vis_hbm.1, bf16[1152,1792]{1,0:T(8,128)(2,1)} %vp_hbm.1, bf16[1792,512]{1,0:T(8,128)(2,1)} %kvp_hbm.1, bf16[112,1792]{1,0:T(8,128)(2,1)} %bitcast.1, bf16[8,1792]{1,0:T(8,128)(2,1)} %q_ref.1, s32[1,2]{1,0:T(1,128)} %range_ref.1, s32[1]{0:T(128)S(6)} %copy.9.lens_ref), custom_call_target="tpu_custom_call" | custom-call | tf_op jit(solution)/shard_map/layer/pallas_call | solution.py:415
  38.4 1.4 %copy.10 = bf16[8,1792]{1,0:T(8,128)(2,1)} copy(bf16[8,1792]{1,0:T(8,128)(2,1)} %layer.1) | data formatting | bytes 57344

commit v3 on v2

--- a/solution.py
+++ b/solution.py
@@ -89,15 +89,20 @@
     own = q_ref.shape[0]
     local = vis.shape[0]
     width = vp.shape[1]
-    chunks = width // COLS
+    starts = [0] + list(range(COLS, width, 2 * COLS))
+    chunks = len(starts)
     blocks = n * own // QBLK
     per_block = QBLK // own
 
     vis_copy = pltpu.make_async_copy(vis_hbm, vis, load_sem.at[0])
     vis_copy.start()
 
+    def chunk_columns(j):
+        stop = starts[j + 1] if j + 1 < chunks else width
+        return pl.ds(starts[j], stop - starts[j])
+
     def vp_copy(j):
-        cols = pl.ds(pl.multiple_of(j * COLS, COLS), COLS)
+        cols = chunk_columns(j)
         return pltpu.make_async_copy(vp_hbm.at[:, cols], vp.at[:, cols], vp_sem.at[j])
 
     vp_copy(0).start()
@@ -128,7 +133,7 @@
 
     def hidden_chunk(j):
         vp_copy(j).wait()
-        cols = pl.ds(pl.multiple_of(j * COLS, COLS), COLS)
+        cols = chunk_columns(j)
         for r in range(local // ROWS):
             rows = pl.ds(r * ROWS, ROWS)
             value = jnp.dot(vis[rows, :], vp[:, cols], preferred_element_type=jnp.float32)
@@ -158,8 +163,7 @@
     w_sibling.start()
     qbuf[me] = q_ref[:, pl.ds(pl.multiple_of(core * HALF, HEAD_DIM), HALF)]
 
-    @pl.loop(1, chunks)
-    def _(j):
+    for j in range(1, chunks):
         hidden_chunk(j)
 
     kvp_copy.wait()
@@ -290,14 +294,19 @@
     def _(i):
         peer = lax.rem(me + i, n)
         s_copy(peer, peer, peer, i).wait_recv()
-        n_copy(peer, peer, peer, i, 0).wait_recv()
-        n_copy(peer, peer, peer, i, 1).wait_recv()
 
     length = lens_ref[lax.div(me * own, QBLK)]
     position = lax.rem(me * own, QBLK) + lax.broadcasted_iota(jnp.int32, (own, HEAD_DIM), 0)
     valid = position < length
+    parts = (range(SPLIT), range(SPLIT, GROUP))
+
+    def piece_columns(piece):
+        heads = parts[piece // KV_HEADS]
+        start = (piece % KV_HEADS) * HALF + heads[0] * HEAD_DIM
+        return pl.ds(start, len(heads) * HEAD_DIM)
+
     def a_copy(slot, peer_outer, index, part):
-        cols = pl.ds(part * HALF, HALF)
+        cols = piece_columns(part)
         return remote(
             attn.at[slot, :, cols],
             attn.at[slot, :, cols],
@@ -306,6 +315,7 @@
             peer_outer * INNER + inner,
         )
 
+    scaled = []
     for k in range(KV_HEADS):
         sources = range(k, n, KV_HEADS)
         top = functools.reduce(jnp.maximum, [statrecv[s] for s in sources])
@@ -317,34 +327,45 @@
                 for f, s in zip(factors, sources)
             ],
         )
-        for h in range(GROUP):
-            cols = pl.ds(h * HEAD_DIM, HEAD_DIM)
-            sums = functools.reduce(
-                jnp.add,
-                [
-                    numrecv[s, :, cols].astype(jnp.float32) * f[:, h : h + 1]
-                    for f, s in zip(factors, sources)
-                ],
-            )
-            normed = jnp.where(valid, sums / totals[:, h : h + 1], 0.0)
-            attn[outer, :, pl.ds(k * HALF + h * HEAD_DIM, HEAD_DIM)] = normed.astype(
-                jnp.bfloat16
-            )
-        for i in range(1, outers):
-            a_copy(outer, lax.rem(outer + i, outers), i, k).start()
+        scaled.append((factors, totals))
+
+    for part, heads in enumerate(parts):
+
+        @pl.loop(1, n)
+        def _(i):
+            peer = lax.rem(me + i, n)
+            n_copy(peer, peer, peer, i, part).wait_recv()
+
+        for k in range(KV_HEADS):
+            factors, totals = scaled[k]
+            for h in heads:
+                cols = pl.ds(h * HEAD_DIM, HEAD_DIM)
+                sums = functools.reduce(
+                    jnp.add,
+                    [
+                        numrecv[s, :, cols].astype(jnp.float32) * f[:, h : h + 1]
+                        for f, s in zip(factors, range(k, n, KV_HEADS))
+                    ],
+                )
+                normed = jnp.where(valid, sums / totals[:, h : h + 1], 0.0)
+                attn[outer, :, pl.ds(k * HALF + h * HEAD_DIM, HEAD_DIM)] = normed.astype(
+                    jnp.bfloat16
+                )
+            for i in range(1, outers):
+                a_copy(outer, lax.rem(outer + i, outers), i, part * KV_HEADS + k).start()
 
     w_arrival(sibling_slot).wait_recv()
     w_arrival(last_slot).wait_recv()
     product = None
-    for k in range(KV_HEADS):
+    for k in range(2 * KV_HEADS):
         for i in range(1, outers):
             peer_outer = lax.rem(outer + i, outers)
             a_copy(peer_outer, peer_outer, i, k).wait_recv()
-        cols = pl.ds(k * HALF, HALF)
+        cols = piece_columns(k)
         rows = (
             attn[:, :, cols]
             .astype(jnp.float32)
-            .reshape(outers * own, HALF)
+            .reshape(outers * own, cols.size)
             .astype(jnp.bfloat16)
         )
         terms = [
@@ -389,8 +410,8 @@
 
     for i in range(1, outers):
         peer_outer = lax.rem(outer + i, outers)
-        a_copy(outer, peer_outer, i, 0).wait_send()
-        a_copy(outer, peer_outer, i, 1).wait_send()
+        for k in range(2 * KV_HEADS):
+            a_copy(outer, peer_outer, i, k).wait_send()
         y_copy(peer_outer, peer_outer, peer_outer, i).wait_recv()
     for i in range(1, outers):
         peer_outer = lax.rem(outer + i, outers)
@@ -445,8 +466,8 @@
             dma((2, n)),
             dma((n,)),
             dma((n,)),
-            dma((2, outers)),
-            dma((2, outers)),
+            dma((2 * KV_HEADS, outers)),
+            dma((2 * KV_HEADS, outers)),
             dma((outers,)),
             dma((outers,)),
         ],

time: 40 us -> 38.3 us (0.957)
  Pallas kernels: 37.7 us -> 36.1 us
    pallas_call x1, Pallas kernels: 37.7 us -> 36.1 us  [body(): pl.pallas_call(functools.partial(kernel, n), out_shape=jax.ShapeDtypeStru...]
where the time goes in v3:
time: 38.3 us; the launch traced here: 38.1 us
  Pallas kernels  36.1 us (94%)
  local copies, waits for them, and re-layouts  1.36 us (4%)
  between operations  0.66 us (2%)
    pallas_call x1, Pallas kernels, body(): pl.pallas_call(functools.partial(kernel, n), out_shape=jax.ShapeDtypeStru...  36.1 us
    unnamed x1, local copies, waits for them, and re-layouts  1.36 us

profile of v3, /device:TPU:0, one launch (start us, length us, event | category | flops | bytes accessed | tf_op | source)
XLA Modules:
  0.0 38.1 jit_solution(2466909222662949600)
XLA Ops:
  0.7 36.1 %layer.1 = bf16[8,1792]{1,0:T(8,128)(2,1)} custom-call(bf16[1024,1152]{1,0:T(8,128)(2,1)} %vis_hbm.1, bf16[1152,1792]{1,0:T(8,128)(2,1)} %vp_hbm.1, bf16[1792,512]{1,0:T(8,128)(2,1)} %kvp_hbm.1, bf16[112,1792]{1,0:T(8,128)(2,1)} %bitcast.1, bf16[8,1792]{1,0:T(8,128)(2,1)} %q_ref.1, s32[1,2]{1,0:T(1,128)} %range_ref.1, s32[1]{0:T(128)S(6)} %copy.9.lens_ref), custom_call_target="tpu_custom_call" | custom-call | tf_op jit(solution)/shard_map/layer/pallas_call | solution.py:436
  36.7 1.4 %copy.10 = bf16[8,1792]{1,0:T(8,128)(2,1)} copy(bf16[8,1792]{1,0:T(8,128)(2,1)} %layer.1) | data formatting | bytes 57344

commit v4 on v3

--- a/solution.py
+++ b/solution.py
@@ -23,7 +23,7 @@
 EXP_SCALE = HEAD_DIM ** (-0.5) * math.log2(math.e)
 GELU_SCALE = math.sqrt(2.0 / math.pi)
 GELU_CUBE = 0.044715 * GELU_SCALE
-SPLIT = 4
+SPLIT = 3
 MESH = pl.DeviceIdType.MESH
 
 

time: 38.3 us -> 38.1 us (level)
  no operation moved by 1% of the time
where the time goes in v4:
time: 38.1 us; the launch traced here: 37.8 us
  Pallas kernels  35.8 us (94%)
  local copies, waits for them, and re-layouts  1.36 us (4%)
  between operations  0.66 us (2%)
    pallas_call x1, Pallas kernels, body(): pl.pallas_call(functools.partial(kernel, n), out_shape=jax.ShapeDtypeStru...  35.8 us
    unnamed x1, local copies, waits for them, and re-layouts  1.36 us

profile of v4, /device:TPU:0, one launch (start us, length us, event | category | flops | bytes accessed | tf_op | source)
XLA Modules:
  0.0 37.8 jit_solution(10486094528338427272)
XLA Ops:
  0.7 35.8 %layer.1 = bf16[8,1792]{1,0:T(8,128)(2,1)} custom-call(bf16[1024,1152]{1,0:T(8,128)(2,1)} %vis_hbm.1, bf16[1152,1792]{1,0:T(8,128)(2,1)} %vp_hbm.1, bf16[1792,512]{1,0:T(8,128)(2,1)} %kvp_hbm.1, bf16[112,1792]{1,0:T(8,128)(2,1)} %bitcast.1, bf16[8,1792]{1,0:T(8,128)(2,1)} %q_ref.1, s32[1,2]{1,0:T(1,128)} %range_ref.1, s32[1]{0:T(128)S(6)} %copy.9.lens_ref), custom_call_target="tpu_custom_call" | custom-call | tf_op jit(solution)/shard_map/layer/pallas_call | solution.py:436
  36.4 1.4 %copy.10 = bf16[8,1792]{1,0:T(8,128)(2,1)} copy(bf16[8,1792]{1,0:T(8,128)(2,1)} %layer.1) | data formatting | bytes 57344
